TPU v7x, 32 devices: a whole 2x2x4 slice. The times are simulated.
32 devices in a mesh: blk: 8 (over y, x, core), rows: 4 (over z).
Axes of the slice: x: 2, y: 2, z: 4, core: 2. Of those that a mesh axis runs over, the one named last changes fastest.
Arguments:
- cholesky: bfloat16 [4096, 256, 256], P('blk', 'rows'), may hold values from -0.01171875 to 0.01171875
- green: bfloat16 [256, 256, 256], P('blk', 'rows'), may hold values from -18 to 18
- aux_field: float32 [256, 4096], P(None, 'blk'), may hold values from -6 to 6
- walker_orbitals: bfloat16 [256, 256, 128], P('blk', 'rows'), may hold values from -6 to 6
Outputs:
- new_orbitals: float32 [256, 256, 128], P('blk', 'rows')
- force_bias: float32 [256, 4096], P(None, 'blk')
All inputs are finite; a program needn't handle non-finite values.
Results may differ from a plain program's by a relative error of at most 0.025.
Values may be sent and summed in bfloat16 or wider, within the bound.
No kernel may reach another device: no remote copies, remote signals or barrier semaphores. Data moves between devices by JAX's collectives and lax.ppermute only.
A program may use at most 128 MiB of HBM per device.

v0:
```python
import jax
import jax.numpy as jnp
from jax import lax
from jax.sharding import PartitionSpec as P

TAYLOR = 4
time_root = 0.5


def shards(cholesky, green, aux_field, walker_orbitals):
    ch_dev, rows_dev, orbitals = cholesky.shape
    flat_chol = cholesky.reshape(ch_dev, rows_dev * orbitals)
    walk_count = walker_orbitals.shape[0]
    batch_piece = lax.all_gather(green, "blk", axis=0, tiled=True)
    flat_piece = batch_piece.reshape(batch_piece.shape[0], rows_dev * orbitals)
    partial_bias = lax.dot_general(
        flat_piece, flat_chol, (((1,), (1,)), ((), ())), preferred_element_type=jnp.float32
    )
    force_bias = lax.psum(partial_bias.astype(jnp.bfloat16), "rows").astype(jnp.float32)
    shifted = (time_root * (aux_field - force_bias)).astype(jnp.bfloat16)
    summed = lax.psum_scatter(
        jnp.dot(shifted, flat_chol, preferred_element_type=jnp.float32).astype(jnp.bfloat16),
        "blk",
        scatter_dimension=0,
        tiled=True,
    )
    potential = summed.reshape(walk_count, rows_dev, orbitals)
    result = walker_orbitals.astype(jnp.float32)
    full_potential = lax.all_gather(potential, "rows", axis=1, tiled=True)
    full_term = lax.all_gather(walker_orbitals, "rows", axis=1, tiled=True)
    offset = lax.axis_index("rows") * rows_dev
    for degree in range(1, TAYLOR + 1):
        product = jnp.einsum(
            "wik,wka->wia", full_potential, full_term, preferred_element_type=jnp.float32
        )
        full_term = (product / degree).astype(jnp.bfloat16)
        own_rows = lax.dynamic_slice_in_dim(full_term, offset, rows_dev, 1)
        result = result + own_rows.astype(jnp.float32)
    return (result, force_bias)


def solution(mesh):
    return jax.shard_map(
        shards,
        mesh=mesh,
        in_specs=(
            P("blk", "rows", None),
            P("blk", "rows", None),
            P(None, "blk"),
            P("blk", "rows", None),
        ),
        out_specs=(P("blk", "rows", None), P(None, "blk")),
        check_vma=False,
    )
```

profile of v0, /device:TPU:0, one launch (start us, length us, event | category | flops | bytes accessed | tf_op | source)
XLA Modules:
  0.0 360.4 jit_solution(13983244792735845269)
XLA Ops:
  7.2 0.0 all-gather.4.cloned.1.call-start
  7.2 2.8 copy.6
  10.0 0.0 all-gather.4.cloned.1.call-update
  10.0 0.0 all-reduce.2.cloned.1.call-start
  10.1 57.4 %all-gather.4.cloned.1.call-done = bf16[256,64,256]{2,0,1:T(8,128)(2,1)} async-done(((bf16[32,64,256]{2,0,1:T(8,128)(2,1)}), bf16[256,64,256]{2,0,1:T(8,128)(2,1)}) %all-gather.4.cloned.1.call-update) | async-done | bytes 8388624 | tf_op jit(solution)/shard_map/all_gather | solution.py:14
  67.5 27.3 %fusion.5 = bf16[256,512]{1,0:T(8,128)(2,1)} fusion(bf16[256,64,256]{2,0,1:T(8,128)(2,1)} %all-gather.4.cloned.1.call-done, bf16[512,64,256]{2,1,0:T(8,128)(2,1)} %param.4), kind=kOutput, calls=%fused_computation.7 | convolution fusion | flops 4295098368 | bytes 25427968 | tf_op jit(solution)/shard_map/dot_general | solution.py:16
  94.7 0.0 reduce-scatter.2.cloned.1.call-start
  94.8 17.9 %copy.8 = bf16[64,8,64,256]{3,1,2,0:T(8,128)(2,1)} copy(bf16[64,8,64,256]{3,2,1,0:T(8,128)(2,1)} %bitcast.19) | data formatting | bytes 33554432
  112.7 17.8 %all-reduce.2.cloned.1.call-done = bf16[256,512]{1,0:T(8,128)(2,1)} async-done(((bf16[256,512]{1,0:T(8,128)(2,1)}), bf16[256,512]{1,0:T(8,128)(2,1)}) %all-reduce.2.cloned.1.call-update) | async-done | bytes 262160 | tf_op jit(solution)/shard_map/psum | solution.py:19
  130.5 1.0 convert_element_type.41
  131.5 12.7 %convolution_convert_fusion = bf16[256,16384]{1,0:T(8,128)(2,1)} fusion(bf16[512,16384]{1,0:T(8,128)(2,1)} %bitcast.18, f32[256,512]{1,0:T(8,128)S(1)} %copy-done.3, f32[256,512]{1,0:T(8,128)S(1)} %convert_element_type.41), kind=kOutput, calls=%fused_computation | convolution fusion | flops 4299554816 | bytes 26214400 | tf_op jit(solution)/shard_map/dot_general | solution.py:22
  144.2 0.0 reduce-scatter.2.cloned.1.call-update
  144.2 0.0 all-gather.8.cloned.1.call-start
  144.3 0.5 all-gather.8.cloned.1.call-update
  144.8 0.3 all-gather.6.cloned.1.call-start
  145.1 70.7 %reduce-scatter.2.cloned.1.call-done = bf16[32,16384]{1,0:T(8,128)(2,1)} async-done(((bf16[256,16384]{1,0:T(8,128)(2,1)}), bf16[32,16384]{1,0:T(8,128)(2,1)}) %reduce-scatter.2.cloned.1.call-update) | async-done | bytes 1048592 | tf_op jit(solution)/shard_map/reduce_scatter | solution.py:21
  215.7 2.4 copy.9
  218.2 44.7 %all-gather.8.cloned.1.call-done = bf16[32,256,128]{2,1,0:T(8,128)(2,1)} async-done(((bf16[32,64,128]{2,1,0:T(8,128)(2,1)}), bf16[32,256,128]{2,1,0:T(8,128)(2,1)}) %all-gather.8.cloned.1.call-update) | async-done | bytes 2097168 | tf_op jit(solution)/shard_map/all_gather | solution.py:30
  262.9 81.6 %all-gather.6.cloned.1.call-done = bf16[32,256,256]{2,1,0:T(8,128)(2,1)} async-done(((bf16[32,64,256]{2,1,0:T(8,128)(2,1)}), bf16[32,256,256]{2,1,0:T(8,128)(2,1)}) %all-gather.6.cloned.1.call-update) | async-done | bytes 4194320 | tf_op jit(solution)/shard_map/all_gather | solution.py:29
  344.4 4.2 %convolution_convert_fusion.1 = bf16[32,256,128]{2,1,0:T(8,128)(2,1)S(1)} fusion(bf16[32,256,256]{2,1,0:T(8,128)(2,1)} %all-gather.6.cloned.1.call-done, bf16[32,256,128]{2,1,0:T(8,128)(2,1)} %all-gather.8.cloned.1.call-done), kind=kOutput, calls=%fused_computation.5 | convolution fusion | flops 537919488 | bytes 8388608 | tf_op jit(solution)/shard_map/wik,wka->wia/dot_general | solution.py:33
  348.7 1.2 multiply_convert_fusion.1
  349.9 1.2 multiply_convert_fusion
  351.2 1.2 fusion.11
  352.5 1.4 convert_add_fusion
  (10 shorter events, 0.1 us)
Async XLA Ops:
  7.2 60.3 %all-gather.4.cloned.1.call-start = ((), (), s32[]{:S(2)}) async-start(), calls=%async_computation.1 | async-start | bytes 9437184 | tf_op jit(solution)/shard_map/all_gather | solution.py:14
  10.0 120.5 %all-reduce.2.cloned.1.call-start = ((), (), s32[]{:S(2)}) async-start(), calls=%async_computation.2 | async-start | bytes 524288 | tf_op jit(solution)/shard_map/psum | solution.py:19
  94.7 121.0 %reduce-scatter.2.cloned.1.call-start = ((), (), s32[]{:S(2)}) async-start(), calls=%async_computation.3 | async-start | bytes 9437184 | tf_op jit(solution)/shard_map/reduce_scatter | solution.py:21
  94.8 36.7 %copy-start.3 = (f32[256,512]{1,0:T(8,128)S(1)}, f32[256,512]{1,0:T(8,128)}, u32[]{:S(2)}) copy-start(f32[256,512]{1,0:T(8,128)} %param.6) | copy-start | bytes 1572868
  131.5 12.7 %copy-start.2 = (f32[256,512]{1,0:T(8,128)}, f32[256,512]{1,0:T(8,128)S(1)}, u32[]{:S(2)}) copy-start(f32[256,512]{1,0:T(8,128)S(1)} %convert_element_type.41) | copy-start | bytes 1572868
  144.2 118.7 %all-gather.8.cloned.1.call-start = ((), (), s32[]{:S(2)}) async-start(), calls=%async_computation.5 | async-start | bytes 2621440 | tf_op jit(solution)/shard_map/all_gather | solution.py:30
  144.8 199.6 %all-gather.6.cloned.1.call-start = ((), (), s32[]{:S(2)}) async-start(), calls=%async_computation.4 | async-start | bytes 5242880 | tf_op jit(solution)/shard_map/all_gather | solution.py:29
  344.4 4.3 %copy-start = (bf16[32,256,256]{2,1,0:T(8,128)(2,1)S(1)}, bf16[32,256,256]{2,1,0:T(8,128)(2,1)}, u32[]{:S(2)}) copy-start(bf16[32,256,256]{2,1,0:T(8,128)(2,1)} %all-gather.6.cloned.1.call-done) | copy-start | bytes 12582916
  351.2 1.3 copy-start.1
Sparse Core Ops, SparseCore 0:
  10.4 56.9 all-gather.3
  94.9 35.5 all-reduce.1
  144.3 71.3 reduce-scatter.1
  217.2 45.6 all-gather.7
  264.9 79.5 all-gather.5
where the time goes:
time: 361 us; the launch traced here: 360 us
  waiting for transfers between devices  273 us (76%)
  matrix products  47.9 us (13%)
  local copies, waits for them, and re-layouts  23.1 us (6%)
  between operations  13.9 us (4%)
    all_gather x1, waiting for transfers between devices, shards(): full_potential = lax.all_gather(potential, 'rows', axis=1, tiled=True)  81.6 us
    reduce_scatter x1, waiting for transfers between devices, shards(): lax.psum_scatter(jnp.dot(shifted, flat_chol, preferred_element_type=jnp.f...  70.7 us
    all_gather x1, waiting for transfers between devices, shards(): batch_piece = lax.all_gather(green, 'blk', axis=0, tiled=True)  57.4 us
    all_gather x1, waiting for transfers between devices, shards(): full_term = lax.all_gather(walker_orbitals, 'rows', axis=1, tiled=True)  44.7 us
    dot_general x1, matrix products, shards(): lax.dot_general(flat_piece, flat_chol, (((1,), (1,)), ((), ())), preferre...  27.3 us
    unnamed x11, local copies, waits for them, and re-layouts  23.1 us
    psum x1, waiting for transfers between devices, shards(): lax.psum(partial_bias.astype(jnp.bfloat16), 'rows').astype(jnp.float32)  17.8 us
    dot_general x1, matrix products, shards(): jnp.dot(shifted, flat_chol, preferred_element_type=jnp.float32)  12.7 us
  transfers between devices with their start and end apart: 5, of which 5 were waited for; matrix products, arithmetic and copies ran while one was open for 6% of the time, Pallas kernels for 0%

commit v1 on v0

--- a/solution.py
+++ b/solution.py
@@ -26,7 +26,12 @@
     )
     potential = summed.reshape(walk_count, rows_dev, orbitals)
     result = walker_orbitals.astype(jnp.float32)
-    full_potential = lax.all_gather(potential, "rows", axis=1, tiled=True)
+    ring = [potential]
+    for hop in range(3):
+        ring.append(lax.ppermute(ring[-1], "rows", [(dev, (dev + 1) % 4) for dev in range(4)]))
+    full_potential = jnp.roll(
+        jnp.concatenate(ring[::-1], axis=1), (lax.axis_index("rows") + 1) * ring[0].shape[1], axis=1
+    )
     full_term = lax.all_gather(walker_orbitals, "rows", axis=1, tiled=True)
     offset = lax.axis_index("rows") * rows_dev
     for degree in range(1, TAYLOR + 1):

time: 361 us -> 361 us (level)
  waiting for transfers between devices: 273 us -> 245 us
  local copies, waits for them, and re-layouts: 23.1 us -> 34.1 us
  starting transfers between devices: 0.42 us -> 10.3 us
  matrix products: 47.9 us -> 54.3 us
    ppermute x0 -> x3, waiting for transfers between devices: none -> 98.5 us  [shards(): lax.ppermute(ring[-1], 'rows', [(dev, (dev + 1) % 4) for dev in range(4)])]
    all_gather x1 -> x0, waiting for transfers between devices: 81.6 us -> none  [shards(): full_potential = lax.all_gather(potential, 'rows', axis=1, tiled=True)]
    all_gather x1, waiting for transfers between devices: 44.7 us -> 0.01 us  [shards(): full_term = lax.all_gather(walker_orbitals, 'rows', axis=1, tiled=True)]
    ppermute x0 -> x3, starting transfers between devices: none -> 10.1 us  [shards(): lax.ppermute(ring[-1], 'rows', [(dev, (dev + 1) % 4) for dev in range(4)])]
    unnamed x11 -> x16, local copies, waits for them, and re-layouts: 23.1 us -> 33.1 us
    dot_general x4, matrix products: 7.96 us -> 14.6 us  [shards(): jnp.einsum('wik,wka->wia', full_potential, full_term, preferred_element_t...]
  transfers between devices with their start and end apart: 5 -> 7, of which waited for: 5 -> 6; matrix products, arithmetic and copies ran while one was open for 6% -> 8% of each run, Pallas kernels for 0% -> 0%
where the time goes in v1:
time: 361 us; the launch traced here: 360 us
  waiting for transfers between devices  245 us (68%)
  matrix products  54.3 us (15%)
  local copies, waits for them, and re-layouts  34.1 us (9%)
  between operations  13.9 us (4%)
  starting transfers between devices  10.3 us (3%)
    ppermute x3, waiting for transfers between devices, shards(): lax.ppermute(ring[-1], 'rows', [(dev, (dev + 1) % 4) for dev in range(4)])  98.5 us
    reduce_scatter x1, waiting for transfers between devices, shards(): lax.psum_scatter(jnp.dot(shifted, flat_chol, preferred_element_type=jnp.f...  71.5 us
    all_gather x1, waiting for transfers between devices, shards(): batch_piece = lax.all_gather(green, 'blk', axis=0, tiled=True)  57.4 us
    unnamed x16, local copies, waits for them, and re-layouts  33.1 us
    dot_general x1, matrix products, shards(): lax.dot_general(flat_piece, flat_chol, (((1,), (1,)), ((), ())), preferre...  27.3 us
    psum x1, waiting for transfers between devices, shards(): lax.psum(partial_bias.astype(jnp.bfloat16), 'rows').astype(jnp.float32)  17.8 us
    dot_general x4, matrix products, shards(): jnp.einsum('wik,wka->wia', full_potential, full_term, preferred_element_t...  14.6 us
    dot_general x1, matrix products, shards(): jnp.dot(shifted, flat_chol, preferred_element_type=jnp.float32)  12.5 us
  transfers between devices with their start and end apart: 7, of which 6 were waited for; matrix products, arithmetic and copies ran while one was open for 8% of the time, Pallas kernels for 0%

profile of v1, /device:TPU:0, one launch (start us, length us, event | category | flops | bytes accessed | tf_op | source)
XLA Modules:
  0.0 360.2 jit_solution(14055277755142115653)
XLA Ops:
  7.2 2.8 copy.6
  10.1 57.4 %all-gather.3.cloned.1.call-done = bf16[256,64,256]{2,0,1:T(8,128)(2,1)} async-done(((bf16[32,64,256]{2,0,1:T(8,128)(2,1)}), bf16[256,64,256]{2,0,1:T(8,128)(2,1)}) %all-gather.3.cloned.1.call-update) | async-done | bytes 8388624 | tf_op jit(solution)/shard_map/all_gather | solution.py:14
  67.5 27.3 %fusion.20 = bf16[256,512]{1,0:T(8,128)(2,1)} fusion(bf16[256,64,256]{2,0,1:T(8,128)(2,1)} %all-gather.3.cloned.1.call-done, bf16[512,64,256]{2,1,0:T(8,128)(2,1)} %param.4), kind=kOutput, calls=%fused_computation.15 | convolution fusion | flops 4295098368 | bytes 25427968 | tf_op jit(solution)/shard_map/dot_general | solution.py:16
  94.8 17.9 %copy.8 = bf16[64,8,64,256]{3,1,2,0:T(8,128)(2,1)} copy(bf16[64,8,64,256]{3,2,1,0:T(8,128)(2,1)} %bitcast.15) | data formatting | bytes 33554432
  112.7 17.8 %all-reduce.2.cloned.1.call-done = bf16[256,512]{1,0:T(8,128)(2,1)} async-done(((bf16[256,512]{1,0:T(8,128)(2,1)}), bf16[256,512]{1,0:T(8,128)(2,1)}) %all-reduce.2.cloned.1.call-update) | async-done | bytes 262160 | tf_op jit(solution)/shard_map/psum | solution.py:19
  132.3 12.5 %convolution_convert_fusion = bf16[256,16384]{1,0:T(8,128)(2,1)} fusion(bf16[512,16384]{1,0:T(8,128)(2,1)} %bitcast.14, f32[256,512]{1,0:T(8,128)S(1)} %copy-done.2, f32[256,512]{1,0:T(8,128)S(1)} %convert_element_type.41), kind=kOutput, calls=%fused_computation | convolution fusion | flops 4299554816 | bytes 26214400 | tf_op jit(solution)/shard_map/dot_general | solution.py:22
  144.8 71.5 %reduce-scatter.2.cloned.1.call-done = bf16[32,16384]{1,0:T(8,128)(2,1)} async-done(((bf16[256,16384]{1,0:T(8,128)(2,1)}), bf16[32,16384]{1,0:T(8,128)(2,1)}) %reduce-scatter.2.cloned.1.call-update) | async-done | bytes 1048592 | tf_op jit(solution)/shard_map/reduce_scatter | solution.py:21
  216.3 1.5 copy.9
  217.8 1.5 collective-permute-start
  219.3 25.0 %collective-permute-done = bf16[32,64,256]{2,1,0:T(8,128)(2,1)S(1)} collective-permute-done((bf16[32,64,256]{2,1,0:T(8,128)(2,1)S(1)}, bf16[32,64,256]{2,1,0:T(8,128)(2,1)S(1)}, u32[]{:S(2)}, u32[]{:S(2)}) %collective-permute-start) | collective-permute-done | bytes 1048608 | tf_op jit(solution)/shard_map/ppermute | solution.py:31
  244.4 40.6 %collective-permute-done.1 = bf16[32,64,256]{2,1,0:T(8,128)(2,1)S(1)} collective-permute-done((bf16[32,64,256]{2,1,0:T(8,128)(2,1)S(1)}, bf16[32,64,256]{2,1,0:T(8,128)(2,1)S(1)}, u32[]{:S(2)}, u32[]{:S(2)}) %collective-permute-start.1) | collective-permute-done | bytes 1048608 | tf_op jit(solution)/shard_map/ppermute | solution.py:31
  285.0 8.5 %collective-permute-start.2 = (bf16[32,64,256]{2,1,0:T(8,128)(2,1)S(1)}, bf16[32,64,256]{2,1,0:T(8,128)(2,1)}, u32[]{:S(2)}, u32[]{:S(2)}) collective-permute-start(bf16[32,64,256]{2,1,0:T(8,128)(2,1)S(1)} %collective-permute-done.1), channel_id=1, source_target_pairs={{0,1},{1,2},{2,3},{3,0},{4,5},{5,6},{6,7},{7,4},{8,9},{9,10},{10,1... | collective-permute-start | bytes 3145736 | tf_op jit(solution)/shard_map/ppermute | solution.py:31
  293.5 32.9 %collective-permute-done.2 = bf16[32,64,256]{2,1,0:T(8,128)(2,1)} collective-permute-done((bf16[32,64,256]{2,1,0:T(8,128)(2,1)S(1)}, bf16[32,64,256]{2,1,0:T(8,128)(2,1)}, u32[]{:S(2)}, u32[]{:S(2)}) %collective-permute-start.2) | collective-permute-done | bytes 1048608 | tf_op jit(solution)/shard_map/ppermute | solution.py:31
  326.4 2.3 constant_dynamic-update-slice_fusion.7
  328.8 1.1 constant_dynamic-update-slice_fusion.6
  329.9 1.1 constant_dynamic-update-slice_fusion.5
  331.0 1.1 constant_dynamic-update-slice_fusion.4
  332.1 2.3 constant_dynamic-update-slice_fusion.3
  334.4 1.1 constant_dynamic-update-slice_fusion.2
  337.6 4.1 %fusion.10 = bf16[32,256,128]{2,1,0:T(8,128)(2,1)S(1)} fusion(bf16[32,256,128]{2,1,0:T(8,128)(2,1)} %all-gather.5.cloned.1.call-done, bf16[32,512,256]{2,1,0:T(8,128)(2,1)} %constant_dynamic-update-slice_fusion, s32[]{:T(128)S(6)} %select_n.20), kind=kOutput, calls=%fused_computation.13 | convolution fusion | flops 537919488 | bytes 8388612 | tf_op jit(solution)/shard_map/wik,wka->wia/dot_general | solution.py:38
  341.8 3.5 multiply_convert_fusion.1
  345.2 3.5 multiply_convert_fusion
  348.8 3.5 fusion.2
  352.2 1.4 convert_add_fusion
  (19 shorter events, 4.2 us)
Async XLA Ops:
  7.2 60.3 %all-gather.3.cloned.1.call-start = ((), (), s32[]{:S(2)}) async-start(), calls=%async_computation.1 | async-start | bytes 9437184 | tf_op jit(solution)/shard_map/all_gather | solution.py:14
  10.0 120.5 %all-reduce.2.cloned.1.call-start = ((), (), s32[]{:S(2)}) async-start(), calls=%async_computation.2 | async-start | bytes 524288 | tf_op jit(solution)/shard_map/psum | solution.py:19
  94.7 121.6 %reduce-scatter.2.cloned.1.call-start = ((), (), s32[]{:S(2)}) async-start(), calls=%async_computation.3 | async-start | bytes 9437184 | tf_op jit(solution)/shard_map/reduce_scatter | solution.py:21
  94.8 37.5 %copy-start.2 = (f32[256,512]{1,0:T(8,128)S(1)}, f32[256,512]{1,0:T(8,128)}, u32[]{:S(2)}) copy-start(f32[256,512]{1,0:T(8,128)} %param.6) | copy-start | bytes 1572868
  131.5 0.8 copy-start.1
  144.8 192.8 %all-gather.5.cloned.1.call-start = ((), (), s32[]{:S(2)}) async-start(), calls=%async_computation.4 | async-start | bytes 2621440 | tf_op jit(solution)/shard_map/all_gather | solution.py:35
  217.8 26.6 %collective-permute-start = (bf16[32,64,256]{2,1,0:T(8,128)(2,1)S(1)}, bf16[32,64,256]{2,1,0:T(8,128)(2,1)S(1)}, u32[]{:S(2)}, u32[]{:S(2)}) collective-permute-start(bf16[32,64,256]{2,1,0:T(8,128)(2,1)S(1)} %bitcast.16), channel_id=1, source_target_pairs={{0,1},{1,2},{2,3},{3,0},{4,5},{5,6},{6,7},{7,4},{8,9},{9,10},{10,1... | collective-permute-start | bytes 3145736 | tf_op jit(solution)/shard_map/ppermute | solution.py:31
  244.4 40.6 %collective-permute-start.1 = (bf16[32,64,256]{2,1,0:T(8,128)(2,1)S(1)}, bf16[32,64,256]{2,1,0:T(8,128)(2,1)S(1)}, u32[]{:S(2)}, u32[]{:S(2)}) collective-permute-start(bf16[32,64,256]{2,1,0:T(8,128)(2,1)S(1)} %collective-permute-done), channel_id=1, source_target_pairs={{0,1},{1,2},{2,3},{3,0},{4,5},{5,6},{6,7},{7,4},{8,9},{9,10},{10,1... | collective-permute-start | bytes 3145736 | tf_op jit(solution)/shard_map/ppermute | solution.py:31
  285.0 41.5 %collective-permute-start.2 = (bf16[32,64,256]{2,1,0:T(8,128)(2,1)S(1)}, bf16[32,64,256]{2,1,0:T(8,128)(2,1)}, u32[]{:S(2)}, u32[]{:S(2)}) collective-permute-start(bf16[32,64,256]{2,1,0:T(8,128)(2,1)S(1)} %collective-permute-done.1), channel_id=1, source_target_pairs={{0,1},{1,2},{2,3},{3,0},{4,5},{5,6},{6,7},{7,4},{8,9},{9,10},{10,1... | collective-permute-start | bytes 3145736 | tf_op jit(solution)/shard_map/ppermute | solution.py:31
  345.2 7.0 %copy-start = (bf16[32,64,128]{2,1,0:T(8,128)(2,1)S(1)}, bf16[32,64,128]{2,1,0:T(8,128)(2,1)}, u32[]{:S(2)}) copy-start(bf16[32,64,128]{2,1,0:T(8,128)(2,1)} %param.7) | copy-start | bytes 1572868
Sparse Core Ops, SparseCore 0:
  10.4 56.9 all-gather.2
  94.9 35.5 all-reduce.1
  144.9 71.3 reduce-scatter.1
  244.5 69.2 all-gather.4
